TPU v7x, 256 devices: a whole 4x4x8 slice. The times are simulated.
256 devices in a mesh: row: 16 (over z_lo, y), col: 16 (over z_hi, x, core).
Axes of the slice: x: 4, y: 4, z: 8 (z_hi: 2, z_lo: 4; z = z_hi * 4 + z_lo), core: 2. Of those that a mesh axis runs over, the one named last changes fastest.
Arguments:
- features: bfloat16 [16384, 512], P(('row', 'col')), may hold values from -6 to 6
- w_first: bfloat16 [512, 512], replicated, may hold values from -0.25 to 0.25
- w_second: bfloat16 [512, 512], replicated, may hold values from -0.25 to 0.25
- block_index: int32 [16, 16, 64], P('row', 'col'), may hold values from 0 to 63, as said below
- block_count: int32 [16, 16], P('row', 'col'), may hold values from 0 to 16, as said below
- block_values: bfloat16 [16, 16, 64, 128, 128], P('row', 'col'), may hold values from -0.15625 to 0.15625
- cotangent: bfloat16 [16384, 512], P(('row', 'col')), may hold values from -0.046875 to 0.046875
Outputs:
- out_second: bfloat16 [16384, 512], P(('row', 'col'))
- grad_first: float32 [512, 512], replicated
- grad_second: float32 [512, 512], replicated
Inputs may be any that keep to these rules, and one draw needn't show every extreme that they name: `block_index`: in each tile the 64 slots name every block position p = r * 8 + c (block row r, block column c of the tile) once, in some order; the first block_count slots are the tile's nonzero blocks and the others are unused. `block_count`: nonzero blocks of each tile; in every draw some tile has exactly 16.
All inputs are finite; a program needn't handle non-finite values.
Results may differ from a plain program's by a relative error of at most 0.0061.
Values may be sent and summed in bfloat16 or wider, within the bound.
A program may use at most 64 MiB of HBM per device.

v0:
```python
import math
import jax
import jax.numpy as jnp
from jax import lax
from jax.sharding import PartitionSpec as P


def activate(v):
    return jax.nn.gelu(v, approximate=True)


def combine(tile_values, slot_index, slot_count, full_panel, flip):
    slots = slot_index.shape[0]
    block_size = tile_values.shape[-1]
    feat_width = full_panel.shape[1]
    in_blocks = full_panel.shape[0] // block_size
    if flip:
        col_blocks = slots // in_blocks
        out_blocks = col_blocks
    else:
        col_blocks = in_blocks
        out_blocks = slots // in_blocks
    group_size = math.gcd(slots, 32)
    panel_blocks = full_panel.reshape(in_blocks, block_size, feat_width)
    targets = jnp.arange(out_blocks, dtype=jnp.int32)
    offsets = jnp.arange(group_size, dtype=jnp.int32)

    def add_group(group_no, total):
        first_slot = group_no * group_size
        slot_ids = lax.dynamic_slice_in_dim(slot_index, first_slot, group_size, 0)
        group_values = lax.dynamic_slice_in_dim(tile_values, first_slot, group_size, 0)
        block_row = slot_ids // col_blocks
        block_col = slot_ids % col_blocks
        if flip:
            picked = panel_blocks[block_row]
            product = jnp.einsum(
                "sab,saf->sbf", group_values, picked, preferred_element_type=jnp.float32
            )
            target = block_col
        else:
            picked = panel_blocks[block_col]
            product = jnp.einsum(
                "sab,sbf->saf", group_values, picked, preferred_element_type=jnp.float32
            )
            target = block_row
        is_live = first_slot + offsets < slot_count
        onehot = ((target[None, :] == targets[:, None]) & is_live[None, :]).astype(jnp.float32)
        return total + jnp.einsum("os,saf->oaf", onehot, product, precision=lax.Precision.HIGHEST)

    groups = (slot_count + group_size - 1) // group_size
    total = lax.fori_loop(
        0, groups, add_group, jnp.zeros((out_blocks, block_size, feat_width), jnp.float32)
    )
    return total.reshape(out_blocks * block_size, feat_width)


def spread_rows(layer_input, tile_values, slot_index, slot_count):
    full_panel = lax.all_gather(layer_input, "row", axis=0, tiled=True)
    partial_value = combine(tile_values, slot_index, slot_count, full_panel, False)
    return lax.psum_scatter(partial_value, "col", scatter_dimension=0, tiled=True)


def spread_cols(layer_input, tile_values, slot_index, slot_count):
    full_panel = lax.all_gather(layer_input, "col", axis=0, tiled=True)
    partial_value = combine(tile_values, slot_index, slot_count, full_panel, True)
    return lax.psum_scatter(partial_value, "row", scatter_dimension=0, tiled=True)


def local(features, w_first, w_second, block_index, block_count, block_values, cotangent):
    slot_index = block_index[0, 0]
    slot_count = block_count[0, 0]
    tile_values = block_values[0, 0]
    first_linear = jnp.dot(features, w_first, preferred_element_type=jnp.float32).astype(
        jnp.bfloat16
    )
    first_sum = spread_cols(first_linear, tile_values, slot_index, slot_count)
    first_value, act_back = jax.vjp(activate, first_sum)
    first_active = first_value.astype(jnp.bfloat16)
    second_linear = jnp.dot(first_active, w_second, preferred_element_type=jnp.float32).astype(
        jnp.bfloat16
    )
    out_second = spread_rows(second_linear, tile_values, slot_index, slot_count).astype(
        jnp.bfloat16
    )
    back_second = spread_cols(cotangent, tile_values, slot_index, slot_count).astype(jnp.bfloat16)
    second_terms = jnp.einsum(
        "nf,ng->fg", first_active, back_second, preferred_element_type=jnp.float32
    )
    back_act = jnp.einsum("ng,fg->nf", back_second, w_second, preferred_element_type=jnp.float32)
    back_first = act_back(back_act)[0].astype(jnp.bfloat16)
    back_linear = spread_rows(back_first, tile_values, slot_index, slot_count).astype(jnp.bfloat16)
    first_terms = jnp.einsum("nf,ng->fg", features, back_linear, preferred_element_type=jnp.float32)
    grad_first, grad_second = lax.psum((first_terms, second_terms), ("row", "col"))
    return (out_second, grad_first, grad_second)


def solution(mesh):
    return jax.shard_map(
        local,
        mesh=mesh,
        in_specs=(
            P(("row", "col"), None),
            P(),
            P(),
            P("row", "col", None),
            P("row", "col"),
            P("row", "col", None, None, None),
            P(("row", "col"), None),
        ),
        out_specs=(P(("row", "col"), None), P(), P()),
        check_vma=False,
    )
```

profile of v0, /device:TPU:2, one launch (start us, length us, event | category | flops | bytes accessed | tf_op | source)
XLA Modules:
  0.0 914.7 jit_solution(1774365751613363130)
XLA Ops:
  7.2 2.0 convolution_convert_fusion.1
  9.3 0.7 all-gather.9.cloned.1.call-update
  10.7 58.8 %all-gather.5.cloned.1.call-done = bf16[1024,512]{1,0:T(8,128)(2,1)} async-done(((bf16[64,512]{1,0:T(8,128)(2,1)}), bf16[1024,512]{1,0:T(8,128)(2,1)}) %all-gather.5.cloned.1.call-update) | async-done | bytes 1048592 | tf_op jit(solution)/shard_map/all_gather | solution.py:64
  69.5 1.7 broadcast.192.clone.1
  71.2 18.2 %while.52 = (s32[]{:T(128)}, f32[8,128,512]{2,0,1:T(8,128)}, s32[]{:T(128)}, s32[64]{0:T(128)}, s32[]{:T(128)}, /*index=5*/bf16[64,128,128]{2,1,0:T(8,128)(2,1)}...) while((s32[]{:T(128)}, f32[8,128,512]{2,0,1:T(8,128)}, ...), condition=%wide.region_1.2_spmd.clone, body=%wide.region_0.1_spmd.clone.sunk | while | flops 738724224 | bytes 42997128 | solution.py:51
  71.2 0.7 and_select_fusion.12
  71.9 0.7 compare_select_fusion.24
  72.6 4.1 gather_fusion
  76.8 3.5 fusion.127
  80.3 0.7 fusion.128
  80.9 8.4 fusion.129
  89.4 4.3 copy.13
  93.8 29.6 %all-gather.9.cloned.1.call-done = bf16[1024,512]{1,0:T(8,128)(2,1)} async-done(((bf16[64,512]{1,0:T(8,128)(2,1)}), bf16[1024,512]{1,0:T(8,128)(2,1)}) %all-gather.9.cloned.1.call-update) | async-done | bytes 1048592 | tf_op jit(solution)/shard_map/all_gather | solution.py:64
  123.4 1.7 broadcast.192.clone.3
  125.1 16.8 %while.54 = (s32[]{:T(128)}, f32[8,128,512]{2,0,1:T(8,128)}, s32[]{:T(128)}, s32[64]{0:T(128)S(1)}, s32[]{:T(128)}, /*index=5*/bf16[64,128,128]{2,1,0:T(8,128)(2...) while((s32[]{:T(128)}, f32[8,128,512]{2,0,1:T(8,128)}, ...), condition=%wide.region_7.8_spmd.clone, body=%wide.region_6.7_spmd.clone.sunk | while | flops 738724224 | bytes 34608496 | solution.py:51
  125.3 4.0 gather_fusion.2
  129.2 3.5 fusion.141
  132.7 0.7 fusion.142
  133.4 8.4 fusion.143
  141.8 4.2 copy.15
  146.1 64.5 %reduce-scatter.5.cloned.1.call-done = f32[64,512]{1,0:T(8,128)} async-done(((f32[1024,512]{1,0:T(8,128)}), f32[64,512]{1,0:T(8,128)}) %reduce-scatter.5.cloned.1.call-update) | async-done | bytes 131088 | tf_op jit(solution)/shard_map/reduce_scatter | solution.py:66
  210.6 87.3 %reduce-scatter.9.cloned.1.call-done = f32[64,512]{1,0:T(8,128)} async-done(((f32[1024,512]{1,0:T(8,128)}), f32[64,512]{1,0:T(8,128)}) %reduce-scatter.9.cloned.1.call-update) | async-done | bytes 131088 | tf_op jit(solution)/shard_map/reduce_scatter | solution.py:66
  297.9 1.9 fusion.78
  299.9 1.7 convolution_convert_fusion
  301.7 75.4 %all-gather.11.cloned.1.call-done = bf16[1024,512]{1,0:T(8,128)(2,1)} async-done(((bf16[64,512]{1,0:T(8,128)(2,1)}), bf16[1024,512]{1,0:T(8,128)(2,1)}) %all-gather.11.cloned.1.call-update) | async-done | bytes 1048592 | tf_op jit(solution)/shard_map/all_gather | solution.py:58
  377.1 1.7 broadcast.192.clone.2
  378.7 16.6 %while.55 = (s32[]{:T(128)}, f32[8,128,512]{2,0,1:T(8,128)}, s32[]{:T(128)}, s32[64]{0:T(128)S(1)}, s32[]{:T(128)}, /*index=5*/bf16[64,128,128]{2,1,0:T(8,128)(2...) while((s32[]{:T(128)}, f32[8,128,512]{2,0,1:T(8,128)}, ...), condition=%wide.region_10.11_spmd.clone, body=%wide.region_9.10_spmd.clone.sunk | while | flops 738724160 | bytes 34608360 | solution.py:51
  378.8 4.0 gather_fusion.3
  382.8 3.4 fusion.148
  386.3 0.7 fusion.149
  386.9 8.4 fusion.150
  395.4 4.2 copy.16
  399.6 58.9 %all-gather.7.cloned.1.call-done = bf16[1024,512]{1,0:T(8,128)(2,1)} async-done(((bf16[64,512]{1,0:T(8,128)(2,1)}), bf16[1024,512]{1,0:T(8,128)(2,1)}) %all-gather.7.cloned.1.call-update) | async-done | bytes 1048592 | tf_op jit(solution)/shard_map/all_gather | solution.py:58
  458.5 1.7 broadcast.192.clone
  460.1 16.6 %while.53 = (s32[]{:T(128)}, f32[8,128,512]{2,0,1:T(8,128)}, s32[]{:T(128)}, s32[64]{0:T(128)S(1)}, s32[]{:T(128)}, /*index=5*/bf16[64,128,128]{2,1,0:T(8,128)(2...) while((s32[]{:T(128)}, f32[8,128,512]{2,0,1:T(8,128)}, ...), condition=%wide.region_4.5_spmd.clone, body=%wide.region_3.4_spmd.clone.sunk | while | flops 738724160 | bytes 34608360 | solution.py:51
  460.2 4.0 gather_fusion.1
  464.2 3.4 fusion.134
  467.7 0.7 fusion.135
  468.3 8.4 fusion.136
  476.8 4.3 copy.14
  481.1 1.3 fusion.80
  482.5 65.9 %reduce-scatter.11.cloned.1.call-done = f32[64,512]{1,0:T(8,128)} async-done(((f32[1024,512]{1,0:T(8,128)}), f32[64,512]{1,0:T(8,128)}) %reduce-scatter.11.cloned.1.call-update) | async-done | bytes 131088 | tf_op jit(solution)/shard_map/reduce_scatter | solution.py:60
  548.4 2.2 convolution_bitcast_fusion
  550.6 85.9 %reduce-scatter.7.cloned.1.call-done = f32[64,512]{1,0:T(8,128)} async-done(((f32[1024,512]{1,0:T(8,128)}), f32[64,512]{1,0:T(8,128)}) %reduce-scatter.7.cloned.1.call-update) | async-done | bytes 131088 | tf_op jit(solution)/shard_map/reduce_scatter | solution.py:60
  636.5 1.5 convert_element_type.28
  638.0 265.3 %all-reduce.3.cloned.1.call-done = (f32[512,512]{0,1:T(8,128)}, f32[512,512]{1,0:T(8,128)}) async-done(((f32[512,512]{0,1:T(8,128)}, f32[512,512]{1,0:T(8,128)}), (f32[512,512]{0,1:T(8,128)}, f32[512,512]{1,0:T(8,128)})) %all-reduce.3.cloned.1.call-update) | async-done | bytes 2097168 | tf_op jit(solution)/shard_map/psum | solution.py:93
  903.3 2.5 copy.17
  905.9 2.3 copy.73
  (43 shorter events, 0.9 us)
Async XLA Ops:
  7.2 290.7 %copy-start = (bf16[512,512]{1,0:T(8,128)(2,1)S(1)}, bf16[512,512]{1,0:T(8,128)(2,1)}, u32[]{:S(2)}) copy-start(bf16[512,512]{1,0:T(8,128)(2,1)} %param.17) | copy-start | bytes 1572868
  7.2 62.3 %all-gather.5.cloned.1.call-start = ((), (), s32[]{:S(2)}) async-start(), calls=%async_computation.4 | async-start | bytes 1114112 | tf_op jit(solution)/shard_map/all_gather | solution.py:64
  9.2 114.2 %all-gather.9.cloned.1.call-start = ((), (), s32[]{:S(2)}) async-start(), calls=%async_computation.8 | async-start | bytes 1114112 | tf_op jit(solution)/shard_map/all_gather | solution.py:64
  10.0 200.6 %reduce-scatter.5.cloned.1.call-start = ((), (), s32[]{:S(2)}) async-start(), calls=%async_computation.5 | async-start | bytes 2228224 | tf_op jit(solution)/shard_map/reduce_scatter | solution.py:66
  72.6 4.2 copy-start.2
  89.4 35.7 %copy-start.3 = (bf16[64,128,128]{2,1,0:T(8,128)(2,1)S(1)}, bf16[64,128,128]{2,1,0:T(8,128)(2,1)}, u32[]{:S(2)}) copy-start(bf16[64,128,128]{2,1,0:T(8,128)(2,1)} %get-tuple-element.970) | copy-start | bytes 6291460
  89.4 35.7 %copy-start.5 = (s32[64]{0:T(128)S(1)}, s32[64]{0:T(128)}, u32[]{:S(2)}) copy-start(s32[64]{0:T(128)} %get-tuple-element.988) | copy-start | bytes 772
  93.7 204.2 %reduce-scatter.9.cloned.1.call-start = ((), (), s32[]{:S(2)}) async-start(), calls=%async_computation.9 | async-start | bytes 2228224 | tf_op jit(solution)/shard_map/reduce_scatter | solution.py:66
  146.0 231.1 %all-gather.11.cloned.1.call-start = ((), (), s32[]{:S(2)}) async-start(), calls=%async_computation.10 | async-start | bytes 1114112 | tf_op jit(solution)/shard_map/all_gather | solution.py:58
  299.8 158.6 %all-gather.7.cloned.1.call-start = ((), (), s32[]{:S(2)}) async-start(), calls=%async_computation.6 | async-start | bytes 1114112 | tf_op jit(solution)/shard_map/all_gather | solution.py:58
  301.7 246.7 %reduce-scatter.11.cloned.1.call-start = ((), (), s32[]{:S(2)}) async-start(), calls=%async_computation.11 | async-start | bytes 2228224 | tf_op jit(solution)/shard_map/reduce_scatter | solution.py:60
  399.6 236.9 %reduce-scatter.7.cloned.1.call-start = ((), (), s32[]{:S(2)}) async-start(), calls=%async_computation.7 | async-start | bytes 2228224 | tf_op jit(solution)/shard_map/reduce_scatter | solution.py:60
  476.8 4.4 copy-start.4
  476.8 4.4 copy-start.7
  476.8 71.6 %copy-start.6 = (bf16[64,512]{1,0:T(8,128)(2,1)S(1)}, bf16[64,512]{1,0:T(8,128)(2,1)}, u32[]{:S(2)}) copy-start(bf16[64,512]{1,0:T(8,128)(2,1)} %param.15) | copy-start | bytes 196612
  481.1 422.3 %all-reduce.3.cloned.1.call-start = ((), (), s32[]{:S(2)}) async-start(), calls=%async_computation.12 | async-start | bytes 4194304 | tf_op jit(solution)/shard_map/psum | solution.py:93
  481.1 427.0 %copy-start.1 = (bf16[512,512]{1,0:T(8,128)(2,1)S(1)}, bf16[512,512]{1,0:T(8,128)(2,1)}, u32[]{:S(2)}) copy-start(bf16[512,512]{1,0:T(8,128)(2,1)} %param.17) | copy-start | bytes 1572868
Sparse Core Ops, SparseCore 0:
  11.3 58.1 all-gather.4
  72.2 51.1 all-gather.8
  126.0 84.6 reduce-scatter.4
  213.0 84.8 reduce-scatter.8
  300.1 76.9 all-gather.10
  379.3 79.1 all-gather.6
  462.7 85.6 reduce-scatter.10
  552.6 83.7 reduce-scatter.6
  642.6 260.7 all-reduce.2
where the time goes:
time: 915 us
  waiting for transfers between devices  792 us (87%)
  matrix products  56.7 us (6%)
  local copies, waits for them, and re-layouts  44.5 us (5%)
  between operations  14.6 us (2%)
    psum x1, waiting for transfers between devices, local(): lax.psum((first_terms, second_terms), ('row', 'col'))  265 us
    reduce_scatter x2, waiting for transfers between devices, spread_cols(): lax.psum_scatter(partial_value, 'row', scatter_dimension=0, tiled=True)  152 us
    reduce_scatter x2, waiting for transfers between devices, spread_rows(): lax.psum_scatter(partial_value, 'col', scatter_dimension=0, tiled=True)  152 us
    all_gather x2, waiting for transfers between devices, spread_rows(): full_panel = lax.all_gather(layer_input, 'row', axis=0, tiled=True)  134 us
    all_gather x2, waiting for transfers between devices, spread_cols(): full_panel = lax.all_gather(layer_input, 'col', axis=0, tiled=True)  88.4 us
    dot_general x4, matrix products, add_group(): jnp.einsum('os,saf->oaf', onehot, product, precision=lax.Precision.HIGHEST)  33.7 us
  transfers between devices with their start and end apart: 9, of which 9 were waited for; matrix products, arithmetic and copies ran while one was open for 11% of the time, Pallas kernels for 0%

commit v1 on v0

--- a/solution.py
+++ b/solution.py
@@ -55,7 +55,9 @@
 
 
 def spread_rows(layer_input, tile_values, slot_index, slot_count):
-    full_panel = lax.all_gather(layer_input, "row", axis=0, tiled=True)
+    full_panel = jnp.concatenate(
+        lax.all_to_all(jnp.stack([layer_input] * lax.axis_size("row")), "row", 0, 0), axis=0
+    )
     partial_value = combine(tile_values, slot_index, slot_count, full_panel, False)
     return lax.psum_scatter(partial_value, "col", scatter_dimension=0, tiled=True)
 

time: 915 us -> 810 us (0.89)
  waiting for transfers between devices: 792 us -> 673 us
  starting transfers between devices: 0.37 us -> 15.8 us
    all_gather x2 -> x0, waiting for transfers between devices: 134 us -> none  [spread_rows(): full_panel = lax.all_gather(layer_input, 'row', axis=0, tiled=True)]
    all_to_all x0 -> x2, waiting for transfers between devices: none -> 16.5 us  [spread_rows(): lax.all_to_all(jnp.stack([layer_input] * lax.axis_size('row')), 'row', 0, 0)]
    all_to_all x0 -> x2, starting transfers between devices: none -> 15.5 us  [spread_rows(): lax.all_to_all(jnp.stack([layer_input] * lax.axis_size('row')), 'row', 0, 0)]
  transfers between devices with their start and end apart: 9 -> 9, of which waited for: 9 -> 8; matrix products, arithmetic and copies ran while one was open for 11% -> 12% of each run, Pallas kernels for 0% -> 0%
where the time goes in v1:
time: 810 us; the launch traced here: 809 us
  waiting for transfers between devices  673 us (83%)
  matrix products  55.2 us (7%)
  local copies, waits for them, and re-layouts  44.2 us (5%)
  starting transfers between devices  15.8 us (2%)
  between operations  14.9 us (2%)
    psum x1, waiting for transfers between devices, local(): lax.psum((first_terms, second_terms), ('row', 'col'))  265 us
    reduce_scatter x2, waiting for transfers between devices, spread_cols(): lax.psum_scatter(partial_value, 'row', scatter_dimension=0, tiled=True)  152 us
    reduce_scatter x2, waiting for transfers between devices, spread_rows(): lax.psum_scatter(partial_value, 'col', scatter_dimension=0, tiled=True)  150 us
    all_gather x2, waiting for transfers between devices, spread_cols(): full_panel = lax.all_gather(layer_input, 'col', axis=0, tiled=True)  88.4 us
    dot_general x4, matrix products, add_group(): jnp.einsum('os,saf->oaf', onehot, product, precision=lax.Precision.HIGHEST)  33.8 us
    while x4, local copies, waits for them, and re-layouts, combine(): lax.fori_loop(0, groups, add_group, jnp.zeros((out_blocks, block_size, fe...  16.9 us
    all_to_all x2, waiting for transfers between devices, spread_rows(): lax.all_to_all(jnp.stack([layer_input] * lax.axis_size('row')), 'row', 0, 0)  16.5 us
  transfers between devices with their start and end apart: 9, of which 8 were waited for; matrix products, arithmetic and copies ran while one was open for 12% of the time, Pallas kernels for 0%

profile of v1, /device:TPU:2, one launch (start us, length us, event | category | flops | bytes accessed | tf_op | source)
XLA Modules:
  0.0 808.9 jit_solution(16226147788096159250)
XLA Ops:
  7.2 2.0 convolution_convert_fusion.1
  9.3 0.7 all-gather.5.cloned.1.call-update
  10.7 58.8 %all-gather.3.cloned.1.call-done = bf16[1024,512]{1,0:T(8,128)(2,1)} async-done(((bf16[64,512]{1,0:T(8,128)(2,1)}), bf16[1024,512]{1,0:T(8,128)(2,1)}) %all-gather.3.cloned.1.call-update) | async-done | bytes 1048592 | tf_op jit(solution)/shard_map/all_gather | solution.py:66
  69.5 1.7 broadcast.196.clone.1
  71.2 18.2 %while.52 = (s32[]{:T(128)}, f32[8,128,512]{2,0,1:T(8,128)}, s32[]{:T(128)}, s32[64]{0:T(128)}, s32[]{:T(128)}, /*index=5*/bf16[64,128,128]{2,1,0:T(8,128)(2,1)}...) while((s32[]{:T(128)}, f32[8,128,512]{2,0,1:T(8,128)}, ...), condition=%wide.region_1.2_spmd.clone, body=%wide.region_0.1_spmd.clone.sunk | while | flops 738724224 | bytes 42997128 | solution.py:51
  71.2 0.7 and_select_fusion.12
  71.9 0.7 compare_select_fusion.24
  72.7 4.1 gather_fusion
  76.8 3.5 fusion.127
  80.3 0.7 fusion.128
  80.9 8.5 %fusion.129 = f32[8,128,512]{2,0,1:T(8,128)} fusion(f32[8,128,512]{2,0,1:T(8,128)} %get-tuple-element.831, f32[32,128,512]{2,1,0:T(8,128)S(1)} %fusion.127, s32[32]{0:T(128)S(1)} %get-tuple-element.791, pred[32]{0:T(512)(128)(4,1)S(1)} %fusion.128), kind=kOutput, calls=%fused_computation.14.clone.1 | convolution fusion | flops 201851392 | bytes 12583072 | tf_op jit(solution)/shard_map/while/body/os,saf->oaf/dot_general | solution.py:48
  89.4 4.3 copy.13
  93.8 29.6 %all-gather.5.cloned.1.call-done = bf16[1024,512]{1,0:T(8,128)(2,1)} async-done(((bf16[64,512]{1,0:T(8,128)(2,1)}), bf16[1024,512]{1,0:T(8,128)(2,1)}) %all-gather.5.cloned.1.call-update) | async-done | bytes 1048592 | tf_op jit(solution)/shard_map/all_gather | solution.py:66
  123.4 1.7 broadcast.196.clone.3
  125.1 16.7 %while.54 = (s32[]{:T(128)}, f32[8,128,512]{2,0,1:T(8,128)}, s32[]{:T(128)}, s32[64]{0:T(128)S(1)}, s32[]{:T(128)}, /*index=5*/bf16[64,128,128]{2,1,0:T(8,128)(2...) while((s32[]{:T(128)}, f32[8,128,512]{2,0,1:T(8,128)}, ...), condition=%wide.region_7.8_spmd.clone, body=%wide.region_6.7_spmd.clone.sunk | while | flops 738724224 | bytes 34608496 | solution.py:51
  125.3 4.0 gather_fusion.2
  129.3 3.5 fusion.141
  132.7 0.7 fusion.142
  133.4 8.4 %fusion.143 = f32[8,128,512]{2,0,1:T(8,128)} fusion(f32[8,128,512]{2,0,1:T(8,128)} %get-tuple-element.897, f32[32,128,512]{2,1,0:T(8,128)S(1)} %fusion.141, s32[32]{0:T(128)S(1)} %get-tuple-element.809, pred[32]{0:T(512)(128)(4,1)S(1)} %fusion.142), kind=kOutput, calls=%fused_computation.54.clone.1 | convolution fusion | flops 201851392 | bytes 12583072 | tf_op jit(solution)/shard_map/while/body/os,saf->oaf/dot_general | solution.py:48
  141.8 4.2 copy.15
  146.0 64.6 %reduce-scatter.5.cloned.1.call-done = f32[64,512]{1,0:T(8,128)} async-done(((f32[1024,512]{1,0:T(8,128)}), f32[64,512]{1,0:T(8,128)}) %reduce-scatter.5.cloned.1.call-update) | async-done | bytes 131088 | tf_op jit(solution)/shard_map/reduce_scatter | solution.py:68
  210.6 87.3 %reduce-scatter.9.cloned.1.call-done = f32[64,512]{1,0:T(8,128)} async-done(((f32[1024,512]{1,0:T(8,128)}), f32[64,512]{1,0:T(8,128)}) %reduce-scatter.9.cloned.1.call-update) | async-done | bytes 131088 | tf_op jit(solution)/shard_map/reduce_scatter | solution.py:68
  297.9 1.3 fusion.78
  299.2 1.1 stack.5
  300.3 3.7 all-to-all-start.1
  304.1 16.5 %all-to-all-done.1 = bf16[16,64,512]{2,1,0:T(8,128)(2,1)S(1)} async-done(((bf16[16,64,512]{2,1,0:T(8,128)(2,1)}), bf16[16,64,512]{2,1,0:T(8,128)(2,1)S(1)}, u32[]{:S(2)}, u32[]{:S(2)}) %all-to-all-start.1) | async-done | bytes 1048608 | tf_op jit(solution)/shard_map/all_to_all | solution.py:59
  320.6 1.1 stack.4
  321.7 11.9 %all-to-all-start = ((bf16[16,64,512]{2,1,0:T(8,128)(2,1)}), bf16[16,64,512]{2,1,0:T(8,128)(2,1)S(1)}, u32[]{:S(2)}, u32[]{:S(2)}) async-start(bf16[16,64,512]{2,1,0:T(8,128)(2,1)} %stack.4), calls=%async_computation.1 | async-start | bytes 2097152 | tf_op jit(solution)/shard_map/all_to_all | solution.py:59
  333.6 1.7 broadcast.196.clone.2
  335.3 15.7 %while.55 = (s32[]{:T(128)}, f32[8,128,512]{2,0,1:T(8,128)}, s32[]{:T(128)}, s32[64]{0:T(128)S(1)}, s32[]{:T(128)}, /*index=5*/bf16[64,128,128]{2,1,0:T(8,128)(2...) while((s32[]{:T(128)}, f32[8,128,512]{2,0,1:T(8,128)}, ...), condition=%wide.region_10.11_spmd.clone, body=%wide.region_9.10_spmd.clone.sunk | while | flops 738724160 | bytes 34608360 | solution.py:51
  335.4 2.8 gather_fusion.3
  338.2 3.8 fusion.148
  342.6 8.4 %fusion.150 = f32[8,128,512]{2,0,1:T(8,128)} fusion(f32[8,128,512]{2,0,1:T(8,128)} %get-tuple-element.930, f32[32,128,512]{2,1,0:T(8,128)S(1)} %fusion.148, s32[32]{0:T(128)S(1)} %get-tuple-element.818, pred[32]{0:T(512)(128)(4,1)S(1)} %fusion.149), kind=kOutput, calls=%fused_computation.74.clone.1 | convolution fusion | flops 201851392 | bytes 12583072 | tf_op jit(solution)/shard_map/while/body/os,saf->oaf/dot_general | solution.py:48
  351.0 4.2 copy.16
  355.2 1.7 broadcast.196.clone
  356.9 15.7 %while.53 = (s32[]{:T(128)}, f32[8,128,512]{2,0,1:T(8,128)}, s32[]{:T(128)}, s32[64]{0:T(128)S(1)}, s32[]{:T(128)}, /*index=5*/bf16[64,128,128]{2,1,0:T(8,128)(2...) while((s32[]{:T(128)}, f32[8,128,512]{2,0,1:T(8,128)}, ...), condition=%wide.region_4.5_spmd.clone, body=%wide.region_3.4_spmd.clone.sunk | while | flops 738724160 | bytes 34608360 | solution.py:51
  357.0 2.8 gather_fusion.1
  359.8 3.7 fusion.134
  364.2 8.4 %fusion.136 = f32[8,128,512]{2,0,1:T(8,128)} fusion(f32[8,128,512]{2,0,1:T(8,128)} %get-tuple-element.864, f32[32,128,512]{2,1,0:T(8,128)S(1)} %fusion.134, s32[32]{0:T(128)S(1)} %get-tuple-element.800, pred[32]{0:T(512)(128)(4,1)S(1)} %fusion.135), kind=kOutput, calls=%fused_computation.34.clone.1 | convolution fusion | flops 201851392 | bytes 12583072 | tf_op jit(solution)/shard_map/while/body/os,saf->oaf/dot_general | solution.py:48
  372.6 4.3 copy.14
  377.0 1.3 fusion.80
  378.3 64.2 %reduce-scatter.11.cloned.1.call-done = f32[64,512]{1,0:T(8,128)} async-done(((f32[1024,512]{1,0:T(8,128)}), f32[64,512]{1,0:T(8,128)}) %reduce-scatter.11.cloned.1.call-update) | async-done | bytes 131088 | tf_op jit(solution)/shard_map/reduce_scatter | solution.py:62
  442.5 2.2 convolution_bitcast_fusion
  444.7 85.7 %reduce-scatter.7.cloned.1.call-done = f32[64,512]{1,0:T(8,128)} async-done(((f32[1024,512]{1,0:T(8,128)}), f32[64,512]{1,0:T(8,128)}) %reduce-scatter.7.cloned.1.call-update) | async-done | bytes 131088 | tf_op jit(solution)/shard_map/reduce_scatter | solution.py:62
  530.4 1.5 convert_element_type.28
  531.9 265.3 %all-reduce.3.cloned.1.call-done = (f32[512,512]{0,1:T(8,128)}, f32[512,512]{1,0:T(8,128)}) async-done(((f32[512,512]{0,1:T(8,128)}, f32[512,512]{1,0:T(8,128)}), (f32[512,512]{0,1:T(8,128)}, f32[512,512]{1,0:T(8,128)})) %all-reduce.3.cloned.1.call-update) | async-done | bytes 2097168 | tf_op jit(solution)/shard_map/psum | solution.py:95
  797.3 2.5 copy.17
  799.8 2.3 copy.73
  (43 shorter events, 2.3 us)
Async XLA Ops:
  7.2 290.7 %copy-start = (bf16[512,512]{1,0:T(8,128)(2,1)S(1)}, bf16[512,512]{1,0:T(8,128)(2,1)}, u32[]{:S(2)}) copy-start(bf16[512,512]{1,0:T(8,128)(2,1)} %param.17) | copy-start | bytes 1572868
  7.2 62.3 %all-gather.3.cloned.1.call-start = ((), (), s32[]{:S(2)}) async-start(), calls=%async_computation.6 | async-start | bytes 1114112 | tf_op jit(solution)/shard_map/all_gather | solution.py:66
  9.2 114.2 %all-gather.5.cloned.1.call-start = ((), (), s32[]{:S(2)}) async-start(), calls=%async_computation.9 | async-start | bytes 1114112 | tf_op jit(solution)/shard_map/all_gather | solution.py:66
  10.0 200.6 %reduce-scatter.5.cloned.1.call-start = ((), (), s32[]{:S(2)}) async-start(), calls=%async_computation.7 | async-start | bytes 2228224 | tf_op jit(solution)/shard_map/reduce_scatter | solution.py:68
  72.6 4.1 copy-start.2
  89.4 35.7 %copy-start.3 = (bf16[64,128,128]{2,1,0:T(8,128)(2,1)S(1)}, bf16[64,128,128]{2,1,0:T(8,128)(2,1)}, u32[]{:S(2)}) copy-start(bf16[64,128,128]{2,1,0:T(8,128)(2,1)} %get-tuple-element.968) | copy-start | bytes 6291460
  89.4 35.7 %copy-start.5 = (s32[64]{0:T(128)S(1)}, s32[64]{0:T(128)}, u32[]{:S(2)}) copy-start(s32[64]{0:T(128)} %get-tuple-element.988) | copy-start | bytes 772
  93.7 204.2 %reduce-scatter.9.cloned.1.call-start = ((), (), s32[]{:S(2)}) async-start(), calls=%async_computation.10 | async-start | bytes 2228224 | tf_op jit(solution)/shard_map/reduce_scatter | solution.py:68
  210.6 93.3 %copy-start.4 = (f32[64,512]{1,0:T(8,128)S(1)}, f32[64,512]{1,0:T(8,128)}, u32[]{:S(2)}) copy-start(f32[64,512]{1,0:T(8,128)} %reduce-scatter.5.cloned.1.call-done) | copy-start | bytes 393220
  300.3 20.4 %all-to-all-start.1 = ((bf16[16,64,512]{2,1,0:T(8,128)(2,1)}), bf16[16,64,512]{2,1,0:T(8,128)(2,1)S(1)}, u32[]{:S(2)}, u32[]{:S(2)}) async-start(bf16[16,64,512]{2,1,0:T(8,128)(2,1)} %stack.5), calls=%async_computation.4 | async-start | bytes 2097152 | tf_op jit(solution)/shard_map/all_to_all | solution.py:59
  321.7 33.5 %all-to-all-start = ((bf16[16,64,512]{2,1,0:T(8,128)(2,1)}), bf16[16,64,512]{2,1,0:T(8,128)(2,1)S(1)}, u32[]{:S(2)}, u32[]{:S(2)}) async-start(bf16[16,64,512]{2,1,0:T(8,128)(2,1)} %stack.4), calls=%async_computation.1 | async-start | bytes 2097152 | tf_op jit(solution)/shard_map/all_to_all | solution.py:59
  333.6 108.9 %reduce-scatter.11.cloned.1.call-start = ((), (), s32[]{:S(2)}) async-start(), calls=%async_computation.11 | async-start | bytes 2228224 | tf_op jit(solution)/shard_map/reduce_scatter | solution.py:62
  355.2 175.2 %reduce-scatter.7.cloned.1.call-start = ((), (), s32[]{:S(2)}) async-start(), calls=%async_computation.8 | async-start | bytes 2228224 | tf_op jit(solution)/shard_map/reduce_scatter | solution.py:62
  372.6 4.3 copy-start.7
  372.6 69.9 %copy-start.6 = (bf16[64,512]{1,0:T(8,128)(2,1)S(1)}, bf16[64,512]{1,0:T(8,128)(2,1)}, u32[]{:S(2)}) copy-start(bf16[64,512]{1,0:T(8,128)(2,1)} %param.15) | copy-start | bytes 196612
  376.9 420.3 %all-reduce.3.cloned.1.call-start = ((), (), s32[]{:S(2)}) async-start(), calls=%async_computation.12 | async-start | bytes 4194304 | tf_op jit(solution)/shard_map/psum | solution.py:95
  377.0 425.1 %copy-start.1 = (bf16[512,512]{1,0:T(8,128)(2,1)S(1)}, bf16[512,512]{1,0:T(8,128)(2,1)}, u32[]{:S(2)}) copy-start(bf16[512,512]{1,0:T(8,128)(2,1)} %param.17) | copy-start | bytes 1572868
Sparse Core Ops, SparseCore 0:
  11.3 58.1 all-gather.2
  72.2 51.1 all-gather.4
  126.0 84.6 reduce-scatter.4
  213.0 84.8 reduce-scatter.8
  355.3 87.1 reduce-scatter.10
  446.6 83.7 reduce-scatter.6
  536.5 260.6 all-reduce.2
